TPU v7x, 128 devices: a whole 4x4x4 slice. The times are simulated.
128 devices in a mesh: space: 32 (over y, x, core), snap: 4 (over z).
Axes of the slice: x: 4, y: 4, z: 4, core: 2. Of those that a mesh axis runs over, the one named last changes fastest.
Arguments:
- owned_x: bfloat16 [4096, 128, 512], P('space', None, 'snap'), may hold values from -600 to 600
- owned_y: bfloat16 [4096, 128, 512], P('space', None, 'snap'), may hold values from -6 to 6
- patch_dest: int32 [4096], P('space'), may hold values from -1 to 2047, as said below
Outputs:
- q_basis: float32 [2048, 128, 512], P('space', 'snap')
- r_factor: float32 [512, 512], replicated
- projection: float32 [512, 512], replicated
Inputs may be any that keep to these rules, and one draw needn't show every extreme that they name: `patch_dest`: every row block 0 to 2047 is named by exactly one slot; -1 marks an empty slot. The 128 slots of one owner (one aligned block of 128 slots) name at most 4 row blocks of any one slab d * 64 to (d + 1) * 64 - 1, and some owner names exactly 4 of every slab.
All inputs are finite; a program needn't handle non-finite values.
Results may differ from a plain program's by a relative error of at most 0.0003.
Values may be sent and summed in bfloat16 or wider, within the bound.
A program may use at most 128 MiB of HBM per device.

v0:
```python
import math
import jax
import jax.numpy as jnp
from jax import lax
from jax.sharding import PartitionSpec as P

PATCH = 128
BLK_DEV = 64


def in_order(pieces, dim):
    pieces = jnp.moveaxis(pieces, 0, dim)
    shape = pieces.shape
    return pieces.reshape(*shape[:dim], shape[dim] * shape[dim + 1], *shape[dim + 2 :])


def from_everyone(array, axis):
    copies = jnp.broadcast_to(array, (lax.axis_size(axis), *array.shape))
    return lax.all_to_all(copies, axis, split_axis=0, concat_axis=0, tiled=True)


def collect(array, axis, dim):
    return in_order(from_everyone(array, axis), dim)


def slab_ranks(destination, per_slab):
    target = jnp.where(destination >= 0, destination // per_slab, -1)
    slot_count = destination.shape[-1]
    same_slab = target[..., :, None] == target[..., None, :]
    before = lax.broadcasted_iota(jnp.int32, (slot_count, slot_count), 1) < lax.broadcasted_iota(
        jnp.int32, (slot_count, slot_count), 0
    )
    order_rank = jnp.sum((same_slab & before).astype(jnp.int32), axis=-1)
    return (target, order_rank)


def send_table(destination, per_slab, slab_count, capacity):
    target, order_rank = slab_ranks(destination, per_slab)
    slot_count = destination.shape[0]
    where_to = jnp.where(target >= 0, target * capacity + order_rank, slab_count * capacity)
    start_table = jnp.full((slab_count * capacity,), slot_count, jnp.int32)
    return start_table.at[where_to].set(jnp.arange(slot_count, dtype=jnp.int32), mode="drop")


def arrival_index(all_lists, per_slab, capacity, my_slab):
    slot_count = all_lists.shape[1]
    target, order_rank = slab_ranks(all_lists, per_slab)
    wanted = my_slab * per_slab + jnp.arange(per_slab, dtype=jnp.int32)
    matches = all_lists.reshape(-1)[None, :] == wanted[:, None]
    located = jnp.argmax(matches, axis=1)
    source = located // slot_count
    return source * capacity + order_rank.reshape(-1)[located]


def pick_rows(payload, indices):
    return jnp.take(payload, indices, axis=0, mode="fill", fill_value=0)


def body(owned_x, owned_y, patch_dest):
    slab_count = lax.axis_size("space")
    slot_count = patch_dest.shape[0]
    capacity = slot_count // slab_count
    my_slab = lax.axis_index("space")
    all_lists = collect(patch_dest, "space", 0)
    outgoing_table = send_table(patch_dest, BLK_DEV, slab_count, capacity)
    received_at = arrival_index(
        all_lists.reshape(slab_count, slot_count), BLK_DEV, capacity, my_slab
    )
    rows_total = slab_count * BLK_DEV * PATCH
    contract = (((0,), (0,)), ((), ()))
    block_x, block_y = (
        lax.all_to_all(owned_x, "snap", split_axis=1, concat_axis=2, tiled=True),
        lax.all_to_all(owned_y, "snap", split_axis=1, concat_axis=2, tiled=True),
    )
    width = block_x.shape[-1]
    used = patch_dest >= 0
    kept_x = jnp.where(used[:, None, None], block_x, jnp.zeros_like(block_x))
    local_cross = lax.dot_general(
        kept_x.reshape(-1, width),
        block_y.reshape(-1, width),
        contract,
        preferred_element_type=jnp.float32,
    )
    moved_x = lax.all_to_all(
        pick_rows(block_x, outgoing_table), "space", split_axis=0, concat_axis=0, tiled=True
    )
    slab_x = jnp.take(moved_x, received_at, axis=0)
    cell_rows = slab_x.reshape(-1, width)
    local_gram = lax.dot_general(cell_rows, cell_rows, contract, preferred_element_type=jnp.float32)
    gram_total, cross_total = lax.psum((local_gram, local_cross), ("space", "snap"))
    identity = jnp.eye(width, dtype=jnp.float32)
    lower = jnp.linalg.cholesky(gram_total / rows_total)
    inverse = lax.linalg.triangular_solve(lower, identity, left_side=True, lower=True)
    basis_rows = jnp.dot(cell_rows.astype(jnp.float32), inverse.T, precision=lax.Precision.HIGHEST)
    projection = jnp.dot(inverse, cross_total, precision=lax.Precision.HIGHEST) / math.sqrt(
        rows_total
    )
    return (basis_rows.reshape(slab_x.shape[0], slab_x.shape[1], width), lower.T, projection)


def solution(mesh):
    in_specs = (P("space", None, "snap"), P("space", None, "snap"), P("space"))
    out_specs = (P("space", "snap", None), P(), P())
    return jax.shard_map(body, mesh=mesh, in_specs=in_specs, out_specs=out_specs, check_vma=False)
```

profile of v0, /device:TPU:1, one launch (start us, length us, event | category | flops | bytes accessed | tf_op | source)
XLA Modules:
  0.0 512.7 jit_solution(7003955340530065894)
XLA Ops:
  8.4 8.6 %all-to-all-start = ((s32[32,1,128]{2,1,0:T(1,128)}), s32[32,1,128]{2,1,0:T(1,128)S(1)}, u32[]{:S(2)}, u32[]{:S(2)}) async-start(s32[32,1,128]{2,1,0:T(1,128)} %broadcast_in_dim.58), calls=%async_computation | async-start | bytes 32768 | tf_op jit(solution)/shard_map/all_to_all | solution.py:19
  17.0 6.9 %copy.48 = bf16[128,128,128]{2,0,1:T(8,128)(2,1)} copy(bf16[128,128,128]{2,1,0:T(8,128)(2,1)} %param.3) | data formatting | bytes 8388608 | tf_op args[0]
  23.9 5.0 all-to-all-start.1
  29.0 6.9 %copy.55 = bf16[128,128,128]{2,0,1:T(8,128)(2,1)} copy(bf16[128,128,128]{2,1,0:T(8,128)(2,1)} %param.4) | data formatting | bytes 8388608 | tf_op args[1]
  35.8 42.1 %all-to-all-done.1 = bf16[128,128,128]{2,0,1:T(8,128)(2,1)} async-done(((bf16[128,128,128]{2,0,1:T(8,128)(2,1)}), bf16[128,128,128]{2,0,1:T(8,128)(2,1)}, u32[]{:S(2)}, u32[]{:S(2)}) %all-to-all-start.1) | async-done | bytes 4194336 | tf_op jit(solution)/shard_map/all_to_all | solution.py:72
  84.0 6.4 %copy.50 = bf16[128,32,4,128]{0,3,2,1:T(8,128)(2,1)} copy(bf16[128,32,4,128]{3,0,1,2:T(8,128)(2,1)} %bitcast.6) | data formatting | bytes 8388608 | tf_op jit(solution)/shard_map/all_to_all | solution.py:72
  90.5 7.9 %copy.51 = bf16[128,32,512]{2,1,0:T(8,128)(2,1)} copy(bf16[128,32,512]{0,2,1:T(8,128)(2,1)} %bitcast.79) | data formatting | bytes 8388608 | tf_op jit(solution)/shard_map/all_to_all | solution.py:72
  98.4 5.0 gather_fusion.1
  108.0 22.3 %all-to-all-done.3 = bf16[128,128,128]{2,0,1:T(8,128)(2,1)} async-done(((bf16[128,128,128]{2,0,1:T(8,128)(2,1)}), bf16[128,128,128]{2,0,1:T(8,128)(2,1)}, u32[]{:S(2)}, u32[]{:S(2)}) %all-to-all-start.3) | async-done | bytes 4194336 | tf_op jit(solution)/shard_map/all_to_all | solution.py:73
  130.3 9.6 %all-to-all-start.2 = ((bf16[128,32,512]{2,1,0:T(8,128)(2,1)}), bf16[128,32,512]{2,1,0:T(8,128)(2,1)}, u32[]{:S(2)}, u32[]{:S(2)}) async-start(bf16[128,32,512]{2,1,0:T(8,128)(2,1)} %broadcast_select_fusion.1), calls=%async_computation.2 | async-start | bytes 8388608 | tf_op jit(solution)/shard_map/all_to_all | solution.py:84
  143.4 4.9 copy.49
  152.9 5.4 %copy.56 = bf16[128,4,32,128]{3,1,2,0:T(4,128)(2,1)S(1)} copy(bf16[128,4,32,128]{3,0,2,1:T(8,128)(2,1)} %bitcast.23) | data formatting | bytes 8388608 | tf_op jit(solution)/shard_map/all_to_all | solution.py:73
  161.9 28.7 %all-to-all-done.2 = bf16[128,32,512]{2,1,0:T(8,128)(2,1)} async-done(((bf16[128,32,512]{2,1,0:T(8,128)(2,1)}), bf16[128,32,512]{2,1,0:T(8,128)(2,1)}, u32[]{:S(2)}, u32[]{:S(2)}) %all-to-all-start.2) | async-done | bytes 4194336 | tf_op jit(solution)/shard_map/all_to_all | solution.py:84
  197.4 147.6 %all-reduce.4.cloned.1.call-done = (f32[512,512]{0,1:T(8,128)}, f32[512,512]{1,0:T(8,128)}) async-done(((f32[512,512]{0,1:T(8,128)}, f32[512,512]{1,0:T(8,128)}), (f32[512,512]{0,1:T(8,128)}, f32[512,512]{1,0:T(8,128)})) %all-reduce.4.cloned.1.call-update) | async-done | bytes 2097168 | tf_op jit(solution)/shard_map/psum | solution.py:90
  348.0 11.7 %cholesky.96 = f32[128,128]{1,0:T(8,128)S(1)} custom-call(f32[128,128]{1,0:T(8,128)S(1)} %cholesky.250), custom_call_target="Cholesky" | custom-call | tf_op jit(solution)/shard_map/jit(cholesky)/cholesky | solution.py:92
  359.8 9.8 %custom-call.30 = f32[1,128,128]{1,2,0:T(8,128)S(1)} custom-call(f32[1,128,128]{2,1,0:T(8,128)S(1)} %get-tuple-element.56), custom_call_target="InvertDiagBlocksLowerTriangular" | custom-call | tf_op jit(solution)/shard_map/jit(cholesky)/cholesky | solution.py:92
  372.4 12.1 %cholesky.201 = f32[128,128]{1,0:T(8,128)S(1)} custom-call(f32[128,128]{1,0:T(8,128)S(1)} %cholesky.254), custom_call_target="Cholesky" | custom-call | tf_op jit(solution)/shard_map/jit(cholesky)/cholesky | solution.py:92
  384.5 9.8 %custom-call.31 = f32[1,128,128]{1,2,0:T(8,128)S(1)} custom-call(f32[1,128,128]{2,1,0:T(8,128)S(1)} %get-tuple-element.53), custom_call_target="InvertDiagBlocksLowerTriangular" | custom-call | tf_op jit(solution)/shard_map/jit(cholesky)/cholesky | solution.py:92
  395.9 11.7 %cholesky.222 = f32[128,128]{1,0:T(8,128)S(1)} custom-call(f32[128,128]{1,0:T(8,128)S(1)} %cholesky.259), custom_call_target="Cholesky" | custom-call | tf_op jit(solution)/shard_map/jit(cholesky)/cholesky | solution.py:92
  408.3 9.8 %custom-call.32 = f32[1,128,128]{1,2,0:T(8,128)S(1)} custom-call(f32[1,128,128]{2,1,0:T(8,128)S(1)} %get-tuple-element.50), custom_call_target="InvertDiagBlocksLowerTriangular" | custom-call | tf_op jit(solution)/shard_map/jit(cholesky)/cholesky | solution.py:92
  419.5 11.9 %cholesky.239 = f32[128,128]{1,0:T(8,128)S(1)} custom-call(f32[128,128]{1,0:T(8,128)S(1)} %convolution_subtract_fusion.5), custom_call_target="Cholesky" | custom-call | tf_op jit(solution)/shard_map/jit(cholesky)/cholesky | solution.py:92
  436.5 13.9 %while.1 = (s32[]{:T(128)}, f32[512,512]{1,0:T(8,128)}, s32[4,2]{0,1:T(2,128)S(1)}, f32[4,128,128]{2,1,0:T(8,128)}, s32[]{:T(128)}) while((s32[]{:T(128)}, f32[512,512]{1,0:T(8,128)}, s32[4,2]{0,1:T(2,128)S(1)}, f32[4,128,128]{2,1,0:T(8,128)}, s32[]{:T(128)}) %tuple.41), condition=%wide.while_cond, body=%wide.while_body.sunk | while | flops 2 | bytes 132705 | solution.py:93
  450.4 40.1 %custom-call.33 = f32[4,128,128]{1,2,0:T(8,128)S(1)} custom-call(f32[4,128,128]{2,1,0:T(8,128)} %get-tuple-element.12), custom_call_target="InvertDiagBlocksLowerTriangular" | custom-call | tf_op jit(solution)/shard_map/triangular_solve | solution.py:93
  496.5 5.1 fusion.5
  (92 shorter events, 66.1 us)
Async XLA Ops:
  8.4 15.5 %all-to-all-start = ((s32[32,1,128]{2,1,0:T(1,128)}), s32[32,1,128]{2,1,0:T(1,128)S(1)}, u32[]{:S(2)}, u32[]{:S(2)}) async-start(s32[32,1,128]{2,1,0:T(1,128)} %broadcast_in_dim.58), calls=%async_computation | async-start | bytes 32768 | tf_op jit(solution)/shard_map/all_to_all | solution.py:19
  23.9 54.0 %all-to-all-start.1 = ((bf16[128,128,128]{2,0,1:T(8,128)(2,1)}), bf16[128,128,128]{2,0,1:T(8,128)(2,1)}, u32[]{:S(2)}, u32[]{:S(2)}) async-start(bf16[128,128,128]{2,0,1:T(8,128)(2,1)} %copy.48), calls=%async_computation.1 | async-start | bytes 8388608 | tf_op jit(solution)/shard_map/all_to_all | solution.py:72
  35.8 47.0 %copy-start.6 = (s32[128]{0:T(128)S(1)}, s32[128]{0:T(128)}, u32[]{:S(2)}) copy-start(s32[128]{0:T(128)} %param.5) | copy-start | bytes 1540
  77.9 52.4 %all-to-all-start.3 = ((bf16[128,128,128]{2,0,1:T(8,128)(2,1)}), bf16[128,128,128]{2,0,1:T(8,128)(2,1)}, u32[]{:S(2)}, u32[]{:S(2)}) async-start(bf16[128,128,128]{2,0,1:T(8,128)(2,1)} %copy.55), calls=%async_computation.3 | async-start | bytes 8388608 | tf_op jit(solution)/shard_map/all_to_all | solution.py:73
  130.3 60.3 %all-to-all-start.2 = ((bf16[128,32,512]{2,1,0:T(8,128)(2,1)}), bf16[128,32,512]{2,1,0:T(8,128)(2,1)}, u32[]{:S(2)}, u32[]{:S(2)}) async-start(bf16[128,32,512]{2,1,0:T(8,128)(2,1)} %broadcast_select_fusion.1), calls=%async_computation.2 | async-start | bytes 8388608 | tf_op jit(solution)/shard_map/all_to_all | solution.py:84
  139.9 205.2 %all-reduce.4.cloned.1.call-start = ((), (), s32[]{:S(2)}) async-start(), calls=%async_computation.4 | async-start | bytes 4194304 | tf_op jit(solution)/shard_map/psum | solution.py:90
  193.5 2.7 copy-start.3
  345.1 1.8 copy-start
  347.1 1.0 copy-start.2
  369.7 121.1 %copy-start.1 = (f32[512,512]{1,0:T(8,128)S(1)}, f32[512,512]{1,0:T(8,128)}, u32[]{:S(2)}) copy-start(f32[512,512]{1,0:T(8,128)} %fusion.18) | copy-start | bytes 3145732
  490.5 5.9 %copy-start.4 = (bf16[64,32,512]{2,1,0:T(8,128)(2,1)S(1)}, bf16[64,32,512]{2,1,0:T(8,128)(2,1)}, u32[]{:S(2)}) copy-start(bf16[64,32,512]{2,1,0:T(8,128)(2,1)} %copy-done.3) | copy-start | bytes 6291460
  496.0 5.5 %copy-start.5 = (f32[512,512]{1,0:T(8,128)S(1)}, f32[512,512]{1,0:T(8,128)}, u32[]{:S(2)}) copy-start(f32[512,512]{1,0:T(8,128)} %get-tuple-element.40) | copy-start | bytes 3145732
Sparse Core Ops, SparseCore 0:
  196.3 148.7 all-reduce.3
where the time goes:
time: 522 us; the launch traced here: 513 us
  waiting for transfers between devices  241 us (46%)
  other arithmetic  131 us (25%)
  local copies, waits for them, and re-layouts  70.2 us (13%)
  starting transfers between devices  28.1 us (5%)
  matrix products  25.6 us (5%)
  between operations  17.2 us (3%)
    psum x1, waiting for transfers between devices, body(): lax.psum((local_gram, local_cross), ('space', 'snap'))  148 us
    another operation x14, other arithmetic, body(): lower = jnp.linalg.cholesky(gram_total / rows_total)  78.9 us
    all_to_all x1, waiting for transfers between devices, body(): lax.all_to_all(owned_x, 'snap', split_axis=1, concat_axis=2, tiled=True)  42.1 us
    another operation x2, other arithmetic, body(): lax.linalg.triangular_solve(lower, identity, left_side=True, lower=True)  40.1 us
    all_to_all x1, waiting for transfers between devices, body(): lax.all_to_all(pick_rows(block_x, outgoing_table), 'space', split_axis=0,...  28.7 us
    all_to_all x1, waiting for transfers between devices, body(): lax.all_to_all(owned_y, 'snap', split_axis=1, concat_axis=2, tiled=True)  22.3 us
    all_to_all x3, local copies, waits for them, and re-layouts, body(): lax.all_to_all(owned_x, 'snap', split_axis=1, concat_axis=2, tiled=True)  19.3 us
    unnamed x17, local copies, waits for them, and re-layouts  16.1 us
  transfers between devices with their start and end apart: 5, of which 4 were waited for; matrix products, arithmetic and copies ran while one was open for 12% of the time, Pallas kernels for 0%

commit v1 on v0

--- a/solution.py
+++ b/solution.py
@@ -1,3 +1,4 @@
+import functools
 import math
 import jax
 import jax.numpy as jnp
@@ -6,6 +7,15 @@
 
 PATCH = 128
 BLK_DEV = 64
+
+
+def define_node_for(v0, named_axis, mesh_dim):
+    for dev_i in (named_axis, mesh_dim):
+        v0 = lax.psum(v0, dev_i)
+    return v0
+
+
+register_the_runs = functools.partial(define_node_for, named_axis="space", mesh_dim="snap")
 
 
 def in_order(pieces, dim):
@@ -87,7 +97,7 @@
     slab_x = jnp.take(moved_x, received_at, axis=0)
     cell_rows = slab_x.reshape(-1, width)
     local_gram = lax.dot_general(cell_rows, cell_rows, contract, preferred_element_type=jnp.float32)
-    gram_total, cross_total = lax.psum((local_gram, local_cross), ("space", "snap"))
+    gram_total, cross_total = register_the_runs((local_gram, local_cross))
     identity = jnp.eye(width, dtype=jnp.float32)
     lower = jnp.linalg.cholesky(gram_total / rows_total)
     inverse = lax.linalg.triangular_solve(lower, identity, left_side=True, lower=True)

time: 522 us -> 539 us (1.033)
  matrix products: 25.6 us -> 35.8 us
  waiting for transfers between devices: 241 us -> 248 us
    psum x1 -> x2, waiting for transfers between devices: 148 us -> 165 us  [define_node_for(): v0 = lax.psum(v0, dev_i)]
    all_to_all x1, waiting for transfers between devices: 28.7 us -> 18.4 us  [body(): lax.all_to_all(pick_rows(block_x, outgoing_table), 'space', split_axis=0,...]
    dot_general x1, matrix products: 3.57 us -> 13.8 us  [body(): lax.dot_general(kept_x.reshape(-1, width), block_y.reshape(-1, width), co...]
  transfers between devices with their start and end apart: 5 -> 6, of which waited for: 4 -> 5; matrix products, arithmetic and copies ran while one was open for 12% -> 14% of each run, Pallas kernels for 0% -> 0%
where the time goes in v1:
time: 539 us; the launch traced here: 530 us
  waiting for transfers between devices  248 us (46%)
  other arithmetic  131 us (24%)
  local copies, waits for them, and re-layouts  70.5 us (13%)
  matrix products  35.8 us (7%)
  starting transfers between devices  28.1 us (5%)
  between operations  17.5 us (3%)
    psum x2, waiting for transfers between devices, define_node_for(): v0 = lax.psum(v0, dev_i)  165 us
    another operation x14, other arithmetic, body(): lower = jnp.linalg.cholesky(gram_total / rows_total)  78.8 us
    all_to_all x1, waiting for transfers between devices, body(): lax.all_to_all(owned_x, 'snap', split_axis=1, concat_axis=2, tiled=True)  42.1 us
    another operation x2, other arithmetic, body(): lax.linalg.triangular_solve(lower, identity, left_side=True, lower=True)  40.1 us
    all_to_all x1, waiting for transfers between devices, body(): lax.all_to_all(owned_y, 'snap', split_axis=1, concat_axis=2, tiled=True)  22.3 us
    all_to_all x3, local copies, waits for them, and re-layouts, body(): lax.all_to_all(owned_x, 'snap', split_axis=1, concat_axis=2, tiled=True)  19.3 us
    all_to_all x1, waiting for transfers between devices, body(): lax.all_to_all(pick_rows(block_x, outgoing_table), 'space', split_axis=0,...  18.4 us
    unnamed x17, local copies, waits for them, and re-layouts  16.1 us
  transfers between devices with their start and end apart: 6, of which 5 were waited for; matrix products, arithmetic and copies ran while one was open for 14% of the time, Pallas kernels for 0%

profile of v1, /device:TPU:1, one launch (start us, length us, event | category | flops | bytes accessed | tf_op | source)
XLA Modules:
  0.0 530.3 jit_solution(18080569921410941893)
XLA Ops:
  8.4 8.6 %all-to-all-start = ((s32[32,1,128]{2,1,0:T(1,128)}), s32[32,1,128]{2,1,0:T(1,128)S(1)}, u32[]{:S(2)}, u32[]{:S(2)}) async-start(s32[32,1,128]{2,1,0:T(1,128)} %broadcast_in_dim.58), calls=%async_computation | async-start | bytes 32768 | tf_op jit(solution)/shard_map/all_to_all | solution.py:29
  17.0 6.9 %copy.48 = bf16[128,128,128]{2,0,1:T(8,128)(2,1)} copy(bf16[128,128,128]{2,1,0:T(8,128)(2,1)} %param.3) | data formatting | bytes 8388608 | tf_op args[0]
  23.9 5.0 all-to-all-start.1
  29.0 6.9 %copy.55 = bf16[128,128,128]{2,0,1:T(8,128)(2,1)} copy(bf16[128,128,128]{2,1,0:T(8,128)(2,1)} %param.4) | data formatting | bytes 8388608 | tf_op args[1]
  35.8 42.1 %all-to-all-done.1 = bf16[128,128,128]{2,0,1:T(8,128)(2,1)} async-done(((bf16[128,128,128]{2,0,1:T(8,128)(2,1)}), bf16[128,128,128]{2,0,1:T(8,128)(2,1)}, u32[]{:S(2)}, u32[]{:S(2)}) %all-to-all-start.1) | async-done | bytes 4194336 | tf_op jit(solution)/shard_map/all_to_all | solution.py:82
  84.0 6.4 %copy.50 = bf16[128,32,4,128]{0,3,2,1:T(8,128)(2,1)} copy(bf16[128,32,4,128]{3,0,1,2:T(8,128)(2,1)} %bitcast.6) | data formatting | bytes 8388608 | tf_op jit(solution)/shard_map/all_to_all | solution.py:82
  90.5 7.9 %copy.51 = bf16[128,32,512]{2,1,0:T(8,128)(2,1)} copy(bf16[128,32,512]{0,2,1:T(8,128)(2,1)} %bitcast.79) | data formatting | bytes 8388608 | tf_op jit(solution)/shard_map/all_to_all | solution.py:82
  108.0 22.3 %all-to-all-done.3 = bf16[128,128,128]{2,0,1:T(8,128)(2,1)} async-done(((bf16[128,128,128]{2,0,1:T(8,128)(2,1)}), bf16[128,128,128]{2,0,1:T(8,128)(2,1)}, u32[]{:S(2)}, u32[]{:S(2)}) %all-to-all-start.3) | async-done | bytes 4194336 | tf_op jit(solution)/shard_map/all_to_all | solution.py:83
  130.3 9.6 %all-to-all-start.2 = ((bf16[128,32,512]{2,1,0:T(8,128)(2,1)}), bf16[128,32,512]{2,1,0:T(8,128)(2,1)}, u32[]{:S(2)}, u32[]{:S(2)}) async-start(bf16[128,32,512]{2,1,0:T(8,128)(2,1)} %broadcast_select_fusion.1), calls=%async_computation.2 | async-start | bytes 8388608 | tf_op jit(solution)/shard_map/all_to_all | solution.py:94
  153.0 5.4 %copy.56 = bf16[128,4,32,128]{3,1,2,0:T(4,128)(2,1)S(1)} copy(bf16[128,4,32,128]{3,0,2,1:T(8,128)(2,1)} %bitcast.23) | data formatting | bytes 8388608 | tf_op jit(solution)/shard_map/all_to_all | solution.py:83
  158.4 13.8 %fusion = f32[512,512]{1,0:T(8,128)} fusion(bf16[512,8,4,128]{3,2,1,0:T(4,128)(2,1)S(1)} %bitcast.81, bf16[512,8,4,128]{3,2,1,0:T(4,128)(2,1)S(1)} %bitcast.80), kind=kOutput, calls=%fused_computation.6 | convolution fusion | flops 2147483648 | bytes 9437184 | tf_op jit(solution)/shard_map/dot_general | solution.py:88
  172.2 18.4 %all-to-all-done.2 = bf16[128,32,512]{2,1,0:T(8,128)(2,1)} async-done(((bf16[128,32,512]{2,1,0:T(8,128)(2,1)}), bf16[128,32,512]{2,1,0:T(8,128)(2,1)}, u32[]{:S(2)}, u32[]{:S(2)}) %all-to-all-start.2) | async-done | bytes 4194336 | tf_op jit(solution)/shard_map/all_to_all | solution.py:94
  196.2 104.9 %all-reduce.6.cloned.1.call-done = (f32[512,512]{0,1:T(8,128)}, f32[512,512]{1,0:T(8,128)}) async-done(((f32[512,512]{0,1:T(8,128)}, f32[512,512]{1,0:T(8,128)}), (f32[512,512]{0,1:T(8,128)}, f32[512,512]{1,0:T(8,128)})) %all-reduce.6.cloned.1.call-update) | async-done | bytes 2097168 | tf_op jit(solution)/shard_map/psum | solution.py:14
  302.4 59.9 %all-reduce.8.cloned.1.call-done = (f32[512,512]{0,1:T(8,128)}, f32[512,512]{1,0:T(8,128)}) async-done(((f32[512,512]{0,1:T(8,128)}, f32[512,512]{1,0:T(8,128)}), (f32[512,512]{0,1:T(8,128)}, f32[512,512]{1,0:T(8,128)})) %all-reduce.8.cloned.1.call-update) | async-done | bytes 2097168 | tf_op jit(solution)/shard_map/psum | solution.py:14
  365.2 11.7 %cholesky.96 = f32[128,128]{1,0:T(8,128)S(1)} custom-call(f32[128,128]{1,0:T(8,128)S(1)} %cholesky.250), custom_call_target="Cholesky" | custom-call | tf_op jit(solution)/shard_map/jit(cholesky)/cholesky | solution.py:102
  377.0 9.8 %custom-call.30 = f32[1,128,128]{1,2,0:T(8,128)S(1)} custom-call(f32[1,128,128]{2,1,0:T(8,128)S(1)} %get-tuple-element.58), custom_call_target="InvertDiagBlocksLowerTriangular" | custom-call | tf_op jit(solution)/shard_map/jit(cholesky)/cholesky | solution.py:102
  389.6 11.7 %cholesky.201 = f32[128,128]{1,0:T(8,128)S(1)} custom-call(f32[128,128]{1,0:T(8,128)S(1)} %cholesky.254), custom_call_target="Cholesky" | custom-call | tf_op jit(solution)/shard_map/jit(cholesky)/cholesky | solution.py:102
  401.3 10.0 %custom-call.31 = f32[1,128,128]{1,2,0:T(8,128)S(1)} custom-call(f32[1,128,128]{2,1,0:T(8,128)S(1)} %get-tuple-element.55), custom_call_target="InvertDiagBlocksLowerTriangular" | custom-call | tf_op jit(solution)/shard_map/jit(cholesky)/cholesky | solution.py:102
  412.9 11.7 %cholesky.222 = f32[128,128]{1,0:T(8,128)S(1)} custom-call(f32[128,128]{1,0:T(8,128)S(1)} %cholesky.259), custom_call_target="Cholesky" | custom-call | tf_op jit(solution)/shard_map/jit(cholesky)/cholesky | solution.py:102
  425.3 9.8 %custom-call.32 = f32[1,128,128]{1,2,0:T(8,128)S(1)} custom-call(f32[1,128,128]{2,1,0:T(8,128)S(1)} %get-tuple-element.52), custom_call_target="InvertDiagBlocksLowerTriangular" | custom-call | tf_op jit(solution)/shard_map/jit(cholesky)/cholesky | solution.py:102
  436.6 11.9 %cholesky.239 = f32[128,128]{1,0:T(8,128)S(1)} custom-call(f32[128,128]{1,0:T(8,128)S(1)} %convolution_subtract_fusion.5), custom_call_target="Cholesky" | custom-call | tf_op jit(solution)/shard_map/jit(cholesky)/cholesky | solution.py:102
  453.6 14.1 %while.1 = (s32[]{:T(128)}, f32[512,512]{1,0:T(8,128)}, s32[4,2]{0,1:T(2,128)S(1)}, f32[4,128,128]{2,1,0:T(8,128)}, s32[]{:T(128)}) while((s32[]{:T(128)}, f32[512,512]{1,0:T(8,128)}, s32[4,2]{0,1:T(2,128)S(1)}, f32[4,128,128]{2,1,0:T(8,128)}, s32[]{:T(128)}) %tuple.41), condition=%wide.while_cond, body=%wide.while_body.sunk | while | flops 2 | bytes 132705 | solution.py:103
  467.8 40.1 %custom-call.33 = f32[4,128,128]{1,2,0:T(8,128)S(1)} custom-call(f32[4,128,128]{2,1,0:T(8,128)} %get-tuple-element.12), custom_call_target="InvertDiagBlocksLowerTriangular" | custom-call | tf_op jit(solution)/shard_map/triangular_solve | solution.py:103
  513.8 5.1 fusion.5
  (95 shorter events, 72.8 us)
Async XLA Ops:
  8.4 15.5 %all-to-all-start = ((s32[32,1,128]{2,1,0:T(1,128)}), s32[32,1,128]{2,1,0:T(1,128)S(1)}, u32[]{:S(2)}, u32[]{:S(2)}) async-start(s32[32,1,128]{2,1,0:T(1,128)} %broadcast_in_dim.58), calls=%async_computation | async-start | bytes 32768 | tf_op jit(solution)/shard_map/all_to_all | solution.py:29
  23.9 54.0 %all-to-all-start.1 = ((bf16[128,128,128]{2,0,1:T(8,128)(2,1)}), bf16[128,128,128]{2,0,1:T(8,128)(2,1)}, u32[]{:S(2)}, u32[]{:S(2)}) async-start(bf16[128,128,128]{2,0,1:T(8,128)(2,1)} %copy.48), calls=%async_computation.1 | async-start | bytes 8388608 | tf_op jit(solution)/shard_map/all_to_all | solution.py:82
  35.8 47.0 %copy-start.6 = (s32[128]{0:T(128)S(1)}, s32[128]{0:T(128)}, u32[]{:S(2)}) copy-start(s32[128]{0:T(128)} %param.5) | copy-start | bytes 1540
  77.9 52.4 %all-to-all-start.3 = ((bf16[128,128,128]{2,0,1:T(8,128)(2,1)}), bf16[128,128,128]{2,0,1:T(8,128)(2,1)}, u32[]{:S(2)}, u32[]{:S(2)}) async-start(bf16[128,128,128]{2,0,1:T(8,128)(2,1)} %copy.55), calls=%async_computation.3 | async-start | bytes 8388608 | tf_op jit(solution)/shard_map/all_to_all | solution.py:83
  130.3 60.3 %all-to-all-start.2 = ((bf16[128,32,512]{2,1,0:T(8,128)(2,1)}), bf16[128,32,512]{2,1,0:T(8,128)(2,1)}, u32[]{:S(2)}, u32[]{:S(2)}) async-start(bf16[128,32,512]{2,1,0:T(8,128)(2,1)} %broadcast_select_fusion.1), calls=%async_computation.2 | async-start | bytes 8388608 | tf_op jit(solution)/shard_map/all_to_all | solution.py:94
  139.9 161.2 %all-reduce.6.cloned.1.call-start = ((), (), s32[]{:S(2)}) async-start(), calls=%async_computation.4 | async-start | bytes 4194304 | tf_op jit(solution)/shard_map/psum | solution.py:14
  193.5 2.7 copy-start.3
  196.2 166.1 %all-reduce.8.cloned.1.call-start = ((), (), s32[]{:S(2)}) async-start(), calls=%async_computation.5 | async-start | bytes 4194304 | tf_op jit(solution)/shard_map/psum | solution.py:14
  362.3 1.8 copy-start
  364.3 1.0 copy-start.2
  386.9 121.3 %copy-start.1 = (f32[512,512]{1,0:T(8,128)S(1)}, f32[512,512]{1,0:T(8,128)}, u32[]{:S(2)}) copy-start(f32[512,512]{1,0:T(8,128)} %fusion.18) | copy-start | bytes 3145732
  507.9 5.9 %copy-start.4 = (bf16[64,32,512]{2,1,0:T(8,128)(2,1)S(1)}, bf16[64,32,512]{2,1,0:T(8,128)(2,1)}, u32[]{:S(2)}) copy-start(bf16[64,32,512]{2,1,0:T(8,128)(2,1)} %copy-done.3) | copy-start | bytes 6291460
  513.4 5.5 %copy-start.5 = (f32[512,512]{1,0:T(8,128)S(1)}, f32[512,512]{1,0:T(8,128)}, u32[]{:S(2)}) copy-start(f32[512,512]{1,0:T(8,128)} %get-tuple-element.42) | copy-start | bytes 3145732
Sparse Core Ops, SparseCore 0:
  196.3 104.8 all-reduce.5
  303.6 58.6 all-reduce.7
